TPU v7x, 256 devices: a whole 4x4x8 slice. The times are simulated.
256 devices in a mesh: blk: 32 (over y_lo, z, core), uly: 8 (over y_hi, x).
Axes of the slice: x: 4, y: 4 (y_hi: 2, y_lo: 2; y = y_hi * 2 + y_lo), z: 8, core: 2. Of those that a mesh axis runs over, the one named last changes fastest.
Arguments:
- tokens: bfloat16 [32768, 5120], P(('blk', 'uly')), may hold values from -6 to 6
- query_base: bfloat16 [32768, 5120], P(('blk', 'uly')), may hold values from -9 to 9
- key_base: bfloat16 [32768, 5120], P(('blk', 'uly')), may hold values from -9 to 9
- value_base: bfloat16 [32768, 5120], P(('blk', 'uly')), may hold values from -6 to 6
- out_grad: bfloat16 [32768, 5120], P(('blk', 'uly')), may hold values from -0.059814453 to 0.059814453
- down_q: bfloat16 [5120, 64], replicated, may hold values from -0.078125 to 0.078125
- up_q: bfloat16 [64, 5120], replicated, may hold values from -0.75 to 0.75
- down_v: bfloat16 [5120, 64], replicated, may hold values from -0.078125 to 0.078125
- up_v: bfloat16 [64, 5120], replicated, may hold values from -0.75 to 0.75
Outputs:
- attended: bfloat16 [32768, 5120], P(('blk', 'uly'))
- grad_down_q: bfloat16 [5120, 64], replicated
- grad_up_q: bfloat16 [64, 5120], P(None, 'uly')
- grad_down_v: bfloat16 [5120, 64], replicated
- grad_up_v: bfloat16 [64, 5120], P(None, 'uly')
All inputs are finite; a program needn't handle non-finite values.
Results may differ from a plain program's by a relative error of at most 0.025.
Values may be sent and summed in bfloat16 or wider, within the bound.
No kernel may reach another device: no remote copies, remote signals or barrier semaphores. Data moves between devices by JAX's collectives and lax.ppermute only.
A program may use at most 128 MiB of HBM per device.

v0:
```python
import jax
import jax.numpy as jnp
from jax import lax
from jax.sharding import PartitionSpec as P

HEAD = 128


def passed_along(block, axis, distance):
    devices = range(lax.axis_size(axis))
    route = [(i - distance, i) for i in devices if i - distance in devices]
    return lax.ppermute(block, axis, route)


def inner(left, right):
    return lax.dot_general(
        left, right, (((0,), (0,)), ((), ())), preferred_element_type=jnp.float32
    )


def head_pass(query, keys, values, upstream, usable, scale):
    scores = jnp.dot(query, keys.T, preferred_element_type=jnp.float32) * scale
    scores = jnp.where(usable[None, :], scores, -jnp.inf)
    top = jnp.max(scores, axis=1, keepdims=True)
    total = jnp.sum(jnp.exp(scores - top), axis=1, keepdims=True)
    probs = jnp.exp(scores - top - jnp.log(total)).astype(jnp.bfloat16)
    attended = jnp.dot(probs, values, preferred_element_type=jnp.float32).astype(jnp.bfloat16)
    delta = jnp.sum(
        upstream.astype(jnp.float32) * attended.astype(jnp.float32), axis=1, keepdims=True
    )
    prob_grad = jnp.dot(upstream, values.T, preferred_element_type=jnp.float32)
    score_grad = (probs.astype(jnp.float32) * (prob_grad - delta)).astype(jnp.bfloat16)
    query_grad = (jnp.dot(score_grad, keys, preferred_element_type=jnp.float32) * scale).astype(
        jnp.bfloat16
    )
    value_terms = jnp.dot(probs.T, upstream, preferred_element_type=jnp.float32)
    return (attended, query_grad, value_terms)


def per_device(tokens, query_base, key_base, value_base, out_grad, down_q, up_q, down_v, up_v):
    low_q = jnp.dot(tokens, down_q, preferred_element_type=jnp.float32).astype(jnp.bfloat16)
    low_v = jnp.dot(tokens, down_v, preferred_element_type=jnp.float32).astype(jnp.bfloat16)
    query = (
        query_base.astype(jnp.float32) + jnp.dot(low_q, up_q, preferred_element_type=jnp.float32)
    ).astype(jnp.bfloat16)
    value = (
        value_base.astype(jnp.float32) + jnp.dot(low_v, up_v, preferred_element_type=jnp.float32)
    ).astype(jnp.bfloat16)
    query_h, keys_h, values_h, upstream_h = (
        lax.all_to_all(query, "uly", split_axis=1, concat_axis=0, tiled=True),
        lax.all_to_all(key_base, "uly", split_axis=1, concat_axis=0, tiled=True),
        lax.all_to_all(value, "uly", split_axis=1, concat_axis=0, tiled=True),
        lax.all_to_all(out_grad, "uly", split_axis=1, concat_axis=0, tiled=True),
    )
    rows = query_h.shape[0]
    width = query_h.shape[1]
    heads_here = width // HEAD
    scale = HEAD ** (-0.5)
    earlier = passed_along(jnp.stack([keys_h, values_h]), "blk", 1)
    keys_all = jnp.concatenate([earlier[0], keys_h], 0)
    values_all = jnp.concatenate([earlier[1], values_h], 0)
    column = jnp.arange(2 * rows)
    usable = jnp.logical_or(column >= rows, lax.axis_index("blk") > 0)

    def per_head(index, carry):
        attended, query_grad, own_terms, prior_terms = carry
        start = index * HEAD
        result = head_pass(
            lax.dynamic_slice_in_dim(query_h, start, HEAD, 1),
            lax.dynamic_slice_in_dim(keys_all, start, HEAD, 1),
            lax.dynamic_slice_in_dim(values_all, start, HEAD, 1),
            lax.dynamic_slice_in_dim(upstream_h, start, HEAD, 1),
            usable,
            scale,
        )
        attended = lax.dynamic_update_slice_in_dim(attended, result[0], start, 1)
        query_grad = lax.dynamic_update_slice_in_dim(query_grad, result[1], start, 1)
        prior_terms = lax.dynamic_update_slice_in_dim(prior_terms, result[2][:rows], start, 1)
        own_terms = lax.dynamic_update_slice_in_dim(own_terms, result[2][rows:], start, 1)
        return (attended, query_grad, own_terms, prior_terms)

    empty_half = jnp.zeros((rows, width), jnp.bfloat16)
    empty_full = jnp.zeros((rows, width), jnp.float32)
    attended_h, query_grad_h, own_terms, prior_terms = lax.fori_loop(
        0, heads_here, per_head, (empty_half, empty_half, empty_full, empty_full)
    )
    returned = passed_along(prior_terms, "blk", -1)
    value_grad_h = (own_terms + returned).astype(jnp.bfloat16)
    rank = down_q.shape[1]
    first_col = lax.axis_index("uly") * width
    attended, query_grad, value_grad = (
        lax.all_to_all(attended_h, "uly", split_axis=0, concat_axis=1, tiled=True),
        lax.all_to_all(query_grad_h, "uly", split_axis=0, concat_axis=1, tiled=True),
        lax.all_to_all(value_grad_h, "uly", split_axis=0, concat_axis=1, tiled=True),
    )
    lowrank = jnp.concatenate(
        [
            jnp.dot(query_grad, up_q.T, preferred_element_type=jnp.float32),
            jnp.dot(value_grad, up_v.T, preferred_element_type=jnp.float32),
        ],
        1,
    ).astype(jnp.bfloat16)
    down_terms = inner(tokens, lowrank)
    up_q_terms = inner(low_q, query_grad)
    up_v_terms = inner(low_v, value_grad)
    down_total, up_q_total, up_v_total = lax.psum(
        (down_terms, up_q_terms, up_v_terms), ("blk", "uly")
    )
    up_q_part = lax.dynamic_slice_in_dim(up_q_total, first_col, width, 1)
    up_v_part = lax.dynamic_slice_in_dim(up_v_total, first_col, width, 1)
    return (
        attended,
        down_total[:, :rank].astype(jnp.bfloat16),
        up_q_part.astype(jnp.bfloat16),
        down_total[:, rank:].astype(jnp.bfloat16),
        up_v_part.astype(jnp.bfloat16),
    )


def solution(mesh):
    return jax.shard_map(
        per_device,
        mesh=mesh,
        in_specs=(
            P(("blk", "uly"), None),
            P(("blk", "uly"), None),
            P(("blk", "uly"), None),
            P(("blk", "uly"), None),
            P(("blk", "uly"), None),
            P(),
            P(),
            P(),
            P(),
        ),
        out_specs=(P(("blk", "uly"), None), P(), P(None, "uly"), P(), P(None, "uly")),
        check_vma=False,
    )
```

profile of v0, /device:TPU:7, one launch (start us, length us, event | category | flops | bytes accessed | tf_op | source)
XLA Modules:
  0.0 464.2 jit_solution(9758977872020225476)
XLA Ops:
  6.5 6.8 %all-to-all-start.2 = ((bf16[128,8,640]{2,0,1:T(8,128)(2,1)}), bf16[128,8,640]{2,0,1:T(8,128)(2,1)S(1)}, u32[]{:S(2)}, u32[]{:S(2)}) async-start(bf16[128,8,640]{2,0,1:T(8,128)(2,1)} %bitcast.90), calls=%async_computation.2 | async-start | bytes 2621440 | tf_op jit(solution)/shard_map/all_to_all | solution.py:52
  15.8 15.6 %all-to-all-done.2 = bf16[128,8,640]{2,0,1:T(8,128)(2,1)S(1)} async-done(((bf16[128,8,640]{2,0,1:T(8,128)(2,1)}), bf16[128,8,640]{2,0,1:T(8,128)(2,1)S(1)}, u32[]{:S(2)}, u32[]{:S(2)}) %all-to-all-start.2) | async-done | bytes 1310752 | tf_op jit(solution)/shard_map/all_to_all | solution.py:52
  31.4 22.6 %all_to_all.133 = bf16[128,8,640]{2,0,1:T(8,128)(2,1)S(1)} all-to-all(bf16[128,8,640]{2,0,1:T(8,128)(2,1)} %bitcast.91), channel_id=1, replica_groups=mesh['blk'=32,'uly'=8] {'uly'}, dimensions={1} | all-to-all | bytes 2621440 | tf_op jit(solution)/shard_map/all_to_all | solution.py:51
  55.8 5.6 %collective-permute-start = (bf16[2,1024,640]{2,1,0:T(8,128)(2,1)}, bf16[2,1024,640]{2,1,0:T(8,128)(2,1)}, u32[]{:S(2)}, u32[]{:S(2)}) collective-permute-start(bf16[2,1024,640]{2,1,0:T(8,128)(2,1)} %pad_maximum_fusion), channel_id=1, source_target_pairs={{0,8},{8,16},{16,24},{24,32},{32,40},{40,48},{48,56},{56,64},{64,7... | collective-permute-start | bytes 7864328 | tf_op jit(solution)/shard_map/ppermute | solution.py:12
  64.0 6.0 %all-to-all-start.3 = ((bf16[128,8,640]{0,2,1:T(8,128)(2,1)}), bf16[128,8,640]{0,2,1:T(8,128)(2,1)}, u32[]{:S(2)}, u32[]{:S(2)}) async-start(bf16[128,8,640]{0,2,1:T(8,128)(2,1)} %bitcast.89), calls=%async_computation.3 | async-start | bytes 2621440 | tf_op jit(solution)/shard_map/all_to_all | solution.py:53
  73.5 34.2 %all-to-all-done.3 = bf16[128,8,640]{0,2,1:T(8,128)(2,1)} async-done(((bf16[128,8,640]{0,2,1:T(8,128)(2,1)}), bf16[128,8,640]{0,2,1:T(8,128)(2,1)}, u32[]{:S(2)}, u32[]{:S(2)}) %all-to-all-start.3) | async-done | bytes 1310752 | tf_op jit(solution)/shard_map/all_to_all | solution.py:53
  107.7 5.8 %all-to-all-start = ((bf16[128,8,640]{2,0,1:T(8,128)(2,1)}), bf16[128,8,640]{2,0,1:T(8,128)(2,1)}, u32[]{:S(2)}, u32[]{:S(2)}) async-start(bf16[128,8,640]{2,0,1:T(8,128)(2,1)} %bitcast.86), calls=%async_computation | async-start | bytes 2621440 | tf_op jit(solution)/shard_map/all_to_all | solution.py:50
  118.1 6.8 %pad_maximum_fusion.1 = (bf16[2048,640]{1,0:T(8,128)(2,1)}, bf16[2048,640]{1,0:T(8,128)(2,1)}) fusion(bf16[1024,640]{1,0:T(8,128)(2,1)S(1)} %bitcast.77, bf16[1024,640]{1,0:T(8,128)(2,1)S(1)} %get-tuple-element.289, bf16[1024,640]{1,0:T(8,128)(2,1)S(1)} %bitcast.75, bf16[1024,640]{1,0:T(8,128)(2,1)S(1)} %get-tuple-element.288), kind=kLoop, calls=%fused_computation.33 | loop fusion | flops 10485760 | bytes 10485760 | tf_op jit(solution)/shard_map/concatenate | solution.py:60
  124.8 6.9 %all-to-all-done = bf16[128,8,640]{2,0,1:T(8,128)(2,1)} async-done(((bf16[128,8,640]{2,0,1:T(8,128)(2,1)}), bf16[128,8,640]{2,0,1:T(8,128)(2,1)}, u32[]{:S(2)}, u32[]{:S(2)}) %all-to-all-start) | async-done | bytes 1310752 | tf_op jit(solution)/shard_map/all_to_all | solution.py:50
  136.3 103.0 %while.20 = (s32[]{:T(128)}, bf16[1024,640]{1,0:T(8,128)(2,1)S(1)}, bf16[1024,640]{1,0:T(8,128)(2,1)}, f32[1024,640]{1,0:T(8,128)}, f32[1024,640]{1,0:T(8,128)},...) while((s32[]{:T(128)}, bf16[1024,640]{1,0:T(8,128)(2,1)S(1)}, ...), condition=%wide.region_4.5_spmd.clone, body=%wide.region_0.4_spmd.clone.sunk | while | flops 2718827520 | bytes 67680992 | solution.py:84
  151.0 5.6 %fusion.68 = bf16[1024,640]{1,0:T(8,128)(2,1)} fusion(bf16[1024,640]{1,0:T(8,128)(2,1)} %get-tuple-element.383, s32[]{:T(128)S(6)} %select_n.43, bf16[1024,2048]{1,0:T(8,128)(2,1)} %copy-done.1, bf16[1024,128]{1,0:T(8,128)(2,1)S(1)} %constant_dynamic-slice_fusion.2, f32[1024]{0:T(1024)S(1)} %get-tuple-element.364, ...), kind=kOutput, calls=%fused_computation.10.clone.1 | convolution fusion | flops 1082392576 | bytes 5772800 | tf_op jit(solution)/shard_map/while/body/eval_jaxpr/dot_general | solution.py:33
  167.8 3.8 multiply_reduce_fusion.2
  171.6 5.6 %fusion.68 = bf16[1024,640]{1,0:T(8,128)(2,1)} fusion(bf16[1024,640]{1,0:T(8,128)(2,1)} %get-tuple-element.383, s32[]{:T(128)S(6)} %select_n.43, bf16[1024,2048]{1,0:T(8,128)(2,1)} %copy-done.1, bf16[1024,128]{1,0:T(8,128)(2,1)S(1)} %constant_dynamic-slice_fusion.2, f32[1024]{0:T(1024)S(1)} %get-tuple-element.364, ...), kind=kOutput, calls=%fused_computation.10.clone.1 | convolution fusion | flops 1082392576 | bytes 5772800 | tf_op jit(solution)/shard_map/while/body/eval_jaxpr/dot_general | solution.py:33
  188.4 3.8 multiply_reduce_fusion.2
  192.2 5.6 %fusion.68 = bf16[1024,640]{1,0:T(8,128)(2,1)} fusion(bf16[1024,640]{1,0:T(8,128)(2,1)} %get-tuple-element.383, s32[]{:T(128)S(6)} %select_n.43, bf16[1024,2048]{1,0:T(8,128)(2,1)} %copy-done.1, bf16[1024,128]{1,0:T(8,128)(2,1)S(1)} %constant_dynamic-slice_fusion.2, f32[1024]{0:T(1024)S(1)} %get-tuple-element.364, ...), kind=kOutput, calls=%fused_computation.10.clone.1 | convolution fusion | flops 1082392576 | bytes 5772800 | tf_op jit(solution)/shard_map/while/body/eval_jaxpr/dot_general | solution.py:33
  209.0 3.8 multiply_reduce_fusion.2
  212.8 5.6 %fusion.68 = bf16[1024,640]{1,0:T(8,128)(2,1)} fusion(bf16[1024,640]{1,0:T(8,128)(2,1)} %get-tuple-element.383, s32[]{:T(128)S(6)} %select_n.43, bf16[1024,2048]{1,0:T(8,128)(2,1)} %copy-done.1, bf16[1024,128]{1,0:T(8,128)(2,1)S(1)} %constant_dynamic-slice_fusion.2, f32[1024]{0:T(1024)S(1)} %get-tuple-element.364, ...), kind=kOutput, calls=%fused_computation.10.clone.1 | convolution fusion | flops 1082392576 | bytes 5772800 | tf_op jit(solution)/shard_map/while/body/eval_jaxpr/dot_general | solution.py:33
  233.4 5.6 %fusion.68 = bf16[1024,640]{1,0:T(8,128)(2,1)} fusion(bf16[1024,640]{1,0:T(8,128)(2,1)} %get-tuple-element.383, s32[]{:T(128)S(6)} %select_n.43, bf16[1024,2048]{1,0:T(8,128)(2,1)} %copy-done.1, bf16[1024,128]{1,0:T(8,128)(2,1)S(1)} %constant_dynamic-slice_fusion.2, f32[1024]{0:T(1024)S(1)} %get-tuple-element.364, ...), kind=kOutput, calls=%fused_computation.10.clone.1 | convolution fusion | flops 1082392576 | bytes 5772800 | tf_op jit(solution)/shard_map/while/body/eval_jaxpr/dot_general | solution.py:33
  241.7 24.9 %all_to_all.134 = bf16[8,128,640]{2,1,0:T(8,128)(2,1)} all-to-all(bf16[8,128,640]{2,1,0:T(8,128)(2,1)} %bitcast.88), channel_id=1, replica_groups=mesh['blk'=32,'uly'=8] {'uly'}, dimensions={0} | all-to-all | bytes 2621440 | tf_op jit(solution)/shard_map/all_to_all | solution.py:93
  266.7 5.5 %all-to-all-start.4 = ((bf16[8,128,640]{2,1,0:T(8,128)(2,1)}), bf16[8,128,640]{2,1,0:T(8,128)(2,1)S(1)}, u32[]{:S(2)}, u32[]{:S(2)}) async-start(bf16[8,128,640]{2,1,0:T(8,128)(2,1)} %bitcast.87), calls=%async_computation.4 | async-start | bytes 2621440 | tf_op jit(solution)/shard_map/all_to_all | solution.py:92
  276.4 12.2 %all-to-all-done.4 = bf16[8,128,640]{2,1,0:T(8,128)(2,1)S(1)} async-done(((bf16[8,128,640]{2,1,0:T(8,128)(2,1)}), bf16[8,128,640]{2,1,0:T(8,128)(2,1)S(1)}, u32[]{:S(2)}, u32[]{:S(2)}) %all-to-all-start.4) | async-done | bytes 1310752 | tf_op jit(solution)/shard_map/all_to_all | solution.py:92
  288.7 7.9 %all-to-all-start.6 = ((bf16[8,128,640]{2,1,0:T(8,128)(2,1)}), bf16[8,128,640]{2,1,0:T(8,128)(2,1)}, u32[]{:S(2)}, u32[]{:S(2)}) async-start(bf16[8,128,640]{2,1,0:T(8,128)(2,1)} %bitcast.93), calls=%async_computation.6 | async-start | bytes 2621440 | tf_op jit(solution)/shard_map/all_to_all | solution.py:94
  305.2 9.5 %all-to-all-done.6 = bf16[8,128,640]{2,1,0:T(8,128)(2,1)} async-done(((bf16[8,128,640]{2,1,0:T(8,128)(2,1)}), bf16[8,128,640]{2,1,0:T(8,128)(2,1)}, u32[]{:S(2)}, u32[]{:S(2)}) %all-to-all-start.6) | async-done | bytes 1310752 | tf_op jit(solution)/shard_map/all_to_all | solution.py:94
  320.5 139.1 %all-reduce.2 = (bf16[5120,128]{0,1:T(8,128)(2,1)}, bf16[64,5120]{1,0:T(8,128)(2,1)S(1)}, bf16[64,5120]{1,0:T(8,128)(2,1)}) all-reduce(f32[5120,128]{0,1:T(8,128)} %convolution_bitcast_fusion, f32[64,5120]{1,0:T(8,128)S(1)} %copy-done.4, f32[64,5120]{1,0:T(8,128)} %fusion.28), channel_id=1, replica_groups=mesh['blk'=32,'uly'=8] {'blk','uly'}, use_global_device_ids=true, to_apply=%region_5.6 | all-reduce | flops 1310720 | bytes 7864320 | tf_op jit(solution)/shard_map/psum | solution.py:106
  (120 shorter events, 113.8 us)
Async XLA Ops:
  0.6 1.3 copy-start
  0.6 3.0 copy-start.10
  6.5 24.9 %all-to-all-start.2 = ((bf16[128,8,640]{2,0,1:T(8,128)(2,1)}), bf16[128,8,640]{2,0,1:T(8,128)(2,1)S(1)}, u32[]{:S(2)}, u32[]{:S(2)}) async-start(bf16[128,8,640]{2,0,1:T(8,128)(2,1)} %bitcast.90), calls=%async_computation.2 | async-start | bytes 2621440 | tf_op jit(solution)/shard_map/all_to_all | solution.py:52
  53.9 1.9 copy-start.2
  55.8 60.1 %collective-permute-start = (bf16[2,1024,640]{2,1,0:T(8,128)(2,1)}, bf16[2,1024,640]{2,1,0:T(8,128)(2,1)}, u32[]{:S(2)}, u32[]{:S(2)}) collective-permute-start(bf16[2,1024,640]{2,1,0:T(8,128)(2,1)} %pad_maximum_fusion), channel_id=1, source_target_pairs={{0,8},{8,16},{16,24},{24,32},{32,40},{40,48},{48,56},{56,64},{64,7... | collective-permute-start | bytes 7864328 | tf_op jit(solution)/shard_map/ppermute | solution.py:12
  64.0 7.8 %copy-start.7 = (bf16[64,5120]{1,0:T(8,128)(2,1)S(1)}, bf16[64,5120]{1,0:T(8,128)(2,1)}, u32[]{:S(2)}) copy-start(bf16[64,5120]{1,0:T(8,128)(2,1)} %param.17) | copy-start | bytes 1966084
  64.0 43.7 %all-to-all-start.3 = ((bf16[128,8,640]{0,2,1:T(8,128)(2,1)}), bf16[128,8,640]{0,2,1:T(8,128)(2,1)}, u32[]{:S(2)}, u32[]{:S(2)}) async-start(bf16[128,8,640]{0,2,1:T(8,128)(2,1)} %bitcast.89), calls=%async_computation.3 | async-start | bytes 2621440 | tf_op jit(solution)/shard_map/all_to_all | solution.py:53
  70.0 1.8 copy-start.11
  107.7 24.0 %all-to-all-start = ((bf16[128,8,640]{2,0,1:T(8,128)(2,1)}), bf16[128,8,640]{2,0,1:T(8,128)(2,1)}, u32[]{:S(2)}, u32[]{:S(2)}) async-start(bf16[128,8,640]{2,0,1:T(8,128)(2,1)} %bitcast.86), calls=%async_computation | async-start | bytes 2621440 | tf_op jit(solution)/shard_map/all_to_all | solution.py:50
  116.0 2.1 copy-start.3
  143.4 2.5 copy-start.1
  164.0 2.5 copy-start.1
  184.6 2.5 copy-start.1
  205.2 2.5 copy-start.1
  225.8 2.5 copy-start.1
  239.3 27.4 %copy-start.6 = (bf16[1024,640]{1,0:T(8,128)(2,1)}, bf16[1024,640]{1,0:T(8,128)(2,1)S(1)}, u32[]{:S(2)}) copy-start(bf16[1024,640]{1,0:T(8,128)(2,1)S(1)} %get-tuple-element.177) | copy-start | bytes 3932164
  239.3 33.3 %collective-permute-start.1 = (f32[1024,640]{1,0:T(8,128)}, f32[1024,640]{1,0:T(8,128)}, u32[]{:S(2)}, u32[]{:S(2)}) collective-permute-start(f32[1024,640]{1,0:T(8,128)} %get-tuple-element.180), channel_id=1, source_target_pairs={{8,0},{16,8},{24,16},{32,24},{40,32},{48,40},{56,48},{64,56},{72,6... | collective-permute-start | bytes 7864328 | tf_op jit(solution)/shard_map/ppermute | solution.py:12
  266.7 22.0 %all-to-all-start.4 = ((bf16[8,128,640]{2,1,0:T(8,128)(2,1)}), bf16[8,128,640]{2,1,0:T(8,128)(2,1)S(1)}, u32[]{:S(2)}, u32[]{:S(2)}) async-start(bf16[8,128,640]{2,1,0:T(8,128)(2,1)} %bitcast.87), calls=%async_computation.4 | async-start | bytes 2621440 | tf_op jit(solution)/shard_map/all_to_all | solution.py:92
  288.7 7.9 %copy-start.5 = (bf16[8,128,640]{2,1,0:T(8,128)(2,1)}, bf16[8,128,640]{2,1,0:T(8,128)(2,1)S(1)}, u32[]{:S(2)}) copy-start(bf16[8,128,640]{2,1,0:T(8,128)(2,1)S(1)} %all-to-all-done.4) | copy-start | bytes 3932164
  288.7 26.1 %all-to-all-start.6 = ((bf16[8,128,640]{2,1,0:T(8,128)(2,1)}), bf16[8,128,640]{2,1,0:T(8,128)(2,1)}, u32[]{:S(2)}, u32[]{:S(2)}) async-start(bf16[8,128,640]{2,1,0:T(8,128)(2,1)} %bitcast.93), calls=%async_computation.6 | async-start | bytes 2621440 | tf_op jit(solution)/shard_map/all_to_all | solution.py:94
  299.9 4.9 %copy-start.8 = (bf16[64,5120]{1,0:T(8,128)(2,1)S(1)}, bf16[64,5120]{1,0:T(8,128)(2,1)}, u32[]{:S(2)}) copy-start(bf16[64,5120]{1,0:T(8,128)(2,1)} %param.17) | copy-start | bytes 1966084
  305.2 11.3 %copy-start.9 = (bf16[64,5120]{1,0:T(8,128)(2,1)S(1)}, bf16[64,5120]{1,0:T(8,128)(2,1)}, u32[]{:S(2)}) copy-start(bf16[64,5120]{1,0:T(8,128)(2,1)} %param.19) | copy-start | bytes 1966084
  318.5 2.0 copy-start.4
where the time goes:
time: 466 us; the launch traced here: 464 us
  blocking collectives  187 us (40%)
  waiting for transfers between devices  78.9 us (17%)
  matrix products  78.2 us (17%)
  local copies, waits for them, and re-layouts  44.3 us (10%)
  starting transfers between devices  40.1 us (9%)
  other arithmetic  34.9 us (7%)
    psum x1, blocking collectives, per_device(): lax.psum((down_terms, up_q_terms, up_v_terms), ('blk', 'uly'))  139 us
    all_to_all x1, waiting for transfers between devices, per_device(): lax.all_to_all(out_grad, 'uly', split_axis=1, concat_axis=0, tiled=True)  34.2 us
    dot_general x5, matrix products, head_pass(): jnp.dot(score_grad, keys, preferred_element_type=jnp.float32) * scale  28.2 us
    all_to_all x1, blocking collectives, per_device(): lax.all_to_all(query_grad_h, 'uly', split_axis=0, concat_axis=1, tiled=True)  24.9 us
    all_to_all x1, blocking collectives, per_device(): lax.all_to_all(key_base, 'uly', split_axis=1, concat_axis=0, tiled=True)  22.6 us
    dot_general x5, matrix products, head_pass(): jnp.dot(probs, values, preferred_element_type=jnp.float32)  19.2 us
    all_to_all x1, waiting for transfers between devices, per_device(): lax.all_to_all(value, 'uly', split_axis=1, concat_axis=0, tiled=True)  15.6 us
    dot_general x5, matrix products, head_pass(): scores = jnp.dot(query, keys.T, preferred_element_type=jnp.float32) * scale  12.8 us
  transfers between devices with their start and end apart: 7, of which 6 were waited for; matrix products, arithmetic and copies ran while one was open for 7% of the time, Pallas kernels for 0%

commit v1 on v0

--- a/solution.py
+++ b/solution.py
@@ -104,7 +104,7 @@
     up_q_terms = inner(low_q, query_grad)
     up_v_terms = inner(low_v, value_grad)
     down_total, up_q_total, up_v_total = lax.psum(
-        (down_terms, up_q_terms, up_v_terms), ("blk", "uly")
+        lax.psum((down_terms, up_q_terms, up_v_terms), "uly"), "blk"
     )
     up_q_part = lax.dynamic_slice_in_dim(up_q_total, first_col, width, 1)
     up_v_part = lax.dynamic_slice_in_dim(up_v_total, first_col, width, 1)

time: 466 us -> 589 us (1.26)
  waiting for transfers between devices: 78.9 us -> 216 us
  blocking collectives: 187 us -> 151 us
  between operations: 0.8 us -> 14.2 us
    psum x0 -> x1, waiting for transfers between devices: none -> 114 us  [per_device(): lax.psum((down_terms, up_q_terms, up_v_terms), 'uly')]
    all_to_all x1 -> x0, blocking collectives: 24.9 us -> none  [per_device(): lax.all_to_all(query_grad_h, 'uly', split_axis=0, concat_axis=1, tiled=True)]
    ppermute x2, waiting for transfers between devices: 0.45 us -> 25 us  [passed_along(): return lax.ppermute(block, axis, route)]
    psum x1, blocking collectives: 139 us -> 128 us  [per_device(): lax.psum(lax.psum((down_terms, up_q_terms, up_v_terms), 'uly'), 'blk')]
    all_to_all x0 -> x1, starting transfers between devices: none -> 5.9 us  [per_device(): lax.all_to_all(query_grad_h, 'uly', split_axis=0, concat_axis=1, tiled=True)]
  transfers between devices with their start and end apart: 7 -> 9, of which waited for: 6 -> 7; matrix products, arithmetic and copies ran while one was open for 7% -> 5% of each run, Pallas kernels for 0% -> 0%
where the time goes in v1:
time: 589 us; the launch traced here: 582 us
  waiting for transfers between devices  216 us (37%)
  blocking collectives  151 us (26%)
  matrix products  78.2 us (13%)
  starting transfers between devices  44.5 us (8%)
  local copies, waits for them, and re-layouts  42 us (7%)
  other arithmetic  35 us (6%)
  between operations  14.2 us (2%)
    psum x1, blocking collectives, per_device(): lax.psum(lax.psum((down_terms, up_q_terms, up_v_terms), 'uly'), 'blk')  128 us
    psum x1, waiting for transfers between devices, per_device(): lax.psum((down_terms, up_q_terms, up_v_terms), 'uly')  114 us
    all_to_all x1, waiting for transfers between devices, per_device(): lax.all_to_all(out_grad, 'uly', split_axis=1, concat_axis=0, tiled=True)  34.2 us
    dot_general x5, matrix products, head_pass(): jnp.dot(score_grad, keys, preferred_element_type=jnp.float32) * scale  28.2 us
    ppermute x2, waiting for transfers between devices, passed_along(): return lax.ppermute(block, axis, route)  25 us
    all_to_all x1, blocking collectives, per_device(): lax.all_to_all(key_base, 'uly', split_axis=1, concat_axis=0, tiled=True)  22.6 us
    dot_general x5, matrix products, head_pass(): jnp.dot(probs, values, preferred_element_type=jnp.float32)  19.2 us
    all_to_all x1, waiting for transfers between devices, per_device(): lax.all_to_all(value, 'uly', split_axis=1, concat_axis=0, tiled=True)  15.6 us
  transfers between devices with their start and end apart: 9, of which 7 were waited for; matrix products, arithmetic and copies ran while one was open for 5% of the time, Pallas kernels for 0%

profile of v1, /device:TPU:7, one launch (start us, length us, event | category | flops | bytes accessed | tf_op | source)
XLA Modules:
  0.0 581.7 jit_solution(11605313608927288274)
XLA Ops:
  13.0 6.8 %all-to-all-start.2 = ((bf16[128,8,640]{2,0,1:T(8,128)(2,1)}), bf16[128,8,640]{2,0,1:T(8,128)(2,1)S(1)}, u32[]{:S(2)}, u32[]{:S(2)}) async-start(bf16[128,8,640]{2,0,1:T(8,128)(2,1)} %bitcast.90), calls=%async_computation.2 | async-start | bytes 2621440 | tf_op jit(solution)/shard_map/all_to_all | solution.py:52
  22.3 15.6 %all-to-all-done.2 = bf16[128,8,640]{2,0,1:T(8,128)(2,1)S(1)} async-done(((bf16[128,8,640]{2,0,1:T(8,128)(2,1)}), bf16[128,8,640]{2,0,1:T(8,128)(2,1)S(1)}, u32[]{:S(2)}, u32[]{:S(2)}) %all-to-all-start.2) | async-done | bytes 1310752 | tf_op jit(solution)/shard_map/all_to_all | solution.py:52
  37.9 22.6 %all_to_all.133 = bf16[128,8,640]{2,0,1:T(8,128)(2,1)S(1)} all-to-all(bf16[128,8,640]{2,0,1:T(8,128)(2,1)} %bitcast.91), channel_id=1, replica_groups=mesh['blk'=32,'uly'=8] {'uly'}, dimensions={1} | all-to-all | bytes 2621440 | tf_op jit(solution)/shard_map/all_to_all | solution.py:51
  62.4 5.6 collective-permute-start
  70.5 6.0 %all-to-all-start.3 = ((bf16[128,8,640]{0,2,1:T(8,128)(2,1)}), bf16[128,8,640]{0,2,1:T(8,128)(2,1)}, u32[]{:S(2)}, u32[]{:S(2)}) async-start(bf16[128,8,640]{0,2,1:T(8,128)(2,1)} %bitcast.89), calls=%async_computation.3 | async-start | bytes 2621440 | tf_op jit(solution)/shard_map/all_to_all | solution.py:53
  80.0 34.2 %all-to-all-done.3 = bf16[128,8,640]{0,2,1:T(8,128)(2,1)} async-done(((bf16[128,8,640]{0,2,1:T(8,128)(2,1)}), bf16[128,8,640]{0,2,1:T(8,128)(2,1)}, u32[]{:S(2)}, u32[]{:S(2)}) %all-to-all-start.3) | async-done | bytes 1310752 | tf_op jit(solution)/shard_map/all_to_all | solution.py:53
  114.2 5.8 all-to-all-start
  124.6 6.7 %pad_maximum_fusion.1 = (bf16[2048,640]{1,0:T(8,128)(2,1)}, bf16[2048,640]{1,0:T(8,128)(2,1)}) fusion(bf16[1024,640]{1,0:T(8,128)(2,1)S(1)} %bitcast.77, bf16[1024,640]{1,0:T(8,128)(2,1)S(1)} %get-tuple-element.292, bf16[1024,640]{1,0:T(8,128)(2,1)S(1)} %bitcast.75, bf16[1024,640]{1,0:T(8,128)(2,1)S(1)} %get-tuple-element.291), kind=kLoop, calls=%fused_computation.33 | loop fusion | flops 10485760 | bytes 10485760 | tf_op jit(solution)/shard_map/concatenate | solution.py:60
  131.3 6.9 %all-to-all-done = bf16[128,8,640]{2,0,1:T(8,128)(2,1)} async-done(((bf16[128,8,640]{2,0,1:T(8,128)(2,1)}), bf16[128,8,640]{2,0,1:T(8,128)(2,1)}, u32[]{:S(2)}, u32[]{:S(2)}) %all-to-all-start) | async-done | bytes 1310752 | tf_op jit(solution)/shard_map/all_to_all | solution.py:50
  142.8 103.0 %while.20 = (s32[]{:T(128)}, bf16[1024,640]{1,0:T(8,128)(2,1)S(1)}, bf16[1024,640]{1,0:T(8,128)(2,1)}, f32[1024,640]{1,0:T(8,128)}, f32[1024,640]{1,0:T(8,128)},...) while((s32[]{:T(128)}, bf16[1024,640]{1,0:T(8,128)(2,1)S(1)}, ...), condition=%wide.region_4.5_spmd.clone, body=%wide.region_0.4_spmd.clone.sunk | while | flops 2718827520 | bytes 67680992 | solution.py:84
  157.5 5.6 fusion.68
  178.1 5.6 fusion.68
  198.6 5.6 fusion.68
  219.3 5.6 fusion.68
  239.9 5.6 fusion.68
  248.2 5.9 %all-to-all-start.5 = ((bf16[8,128,640]{2,1,0:T(8,128)(2,1)}), bf16[8,128,640]{2,1,0:T(8,128)(2,1)S(1)}, u32[]{:S(2)}, u32[]{:S(2)}) async-start(bf16[8,128,640]{2,1,0:T(8,128)(2,1)} %bitcast.88), calls=%async_computation.5 | async-start | bytes 2621440 | tf_op jit(solution)/shard_map/all_to_all | solution.py:93
  254.2 25.0 %collective-permute-done.1 = f32[1024,640]{1,0:T(8,128)} collective-permute-done((f32[1024,640]{1,0:T(8,128)}, f32[1024,640]{1,0:T(8,128)}, u32[]{:S(2)}, u32[]{:S(2)}) %collective-permute-start.1) | collective-permute-done | bytes 2621472 | tf_op jit(solution)/shard_map/ppermute | solution.py:12
  279.1 3.9 add_convert_fusion
  283.0 6.4 %all-to-all-start.6 = ((bf16[8,128,640]{2,1,0:T(8,128)(2,1)}), bf16[8,128,640]{2,1,0:T(8,128)(2,1)}, u32[]{:S(2)}, u32[]{:S(2)}) async-start(bf16[8,128,640]{2,1,0:T(8,128)(2,1)} %bitcast.93), calls=%async_computation.6 | async-start | bytes 2621440 | tf_op jit(solution)/shard_map/all_to_all | solution.py:94
  293.2 7.5 %all-to-all-done.6 = bf16[8,128,640]{2,1,0:T(8,128)(2,1)} async-done(((bf16[8,128,640]{2,1,0:T(8,128)(2,1)}), bf16[8,128,640]{2,1,0:T(8,128)(2,1)}, u32[]{:S(2)}, u32[]{:S(2)}) %all-to-all-start.6) | async-done | bytes 1310752 | tf_op jit(solution)/shard_map/all_to_all | solution.py:94
  306.6 5.6 all-to-all-start.4
  312.1 13.3 %all-to-all-done.4 = bf16[8,128,640]{2,1,0:T(8,128)(2,1)S(1)} async-done(((bf16[8,128,640]{2,1,0:T(8,128)(2,1)}), bf16[8,128,640]{2,1,0:T(8,128)(2,1)S(1)}, u32[]{:S(2)}, u32[]{:S(2)}) %all-to-all-start.4) | async-done | bytes 1310752 | tf_op jit(solution)/shard_map/all_to_all | solution.py:92
  329.3 113.7 %all-reduce.5.cloned.1.call-done = (f32[5120,128]{0,1:T(8,128)}, f32[64,5120]{1,0:T(8,128)}, f32[64,5120]{1,0:T(8,128)}) async-done(((f32[5120,128]{0,1:T(8,128)}, f32[64,5120]{1,0:T(8,128)}, f32[64,5120]{1,0:T(8,128)}), (f32[5120,128]{0,1:T(8,128)}, f32[64,5120]{1,0:T(8,128)}, f32[64,5120]{1,0:T(8,128)})) %all-reduce.5.cloned.1.call-update) | async-done | bytes 5242896 | tf_op jit(solution)/shard_map/psum | solution.py:107
  443.0 128.5 %all-reduce.6 = (bf16[5120,128]{0,1:T(8,128)(2,1)S(1)}, bf16[64,5120]{1,0:T(8,128)(2,1)S(1)}, bf16[64,5120]{1,0:T(8,128)(2,1)}) all-reduce(f32[5120,128]{0,1:T(8,128)} %get-tuple-element.282, f32[64,5120]{1,0:T(8,128)} %get-tuple-element.283, f32[64,5120]{1,0:T(8,128)} %get-tuple-element.284), channel_id=1, replica_groups=mesh['blk'=32,'uly'=8] {'blk'}, use_global_device_ids=true, to_apply=%region_6.7 | all-reduce | flops 1310720 | bytes 7864320 | tf_op jit(solution)/shard_map/psum | solution.py:106
  (122 shorter events, 118.7 us)
Async XLA Ops:
  7.2 1.3 copy-start
  7.2 3.0 copy-start.9
  13.0 24.9 %all-to-all-start.2 = ((bf16[128,8,640]{2,0,1:T(8,128)(2,1)}), bf16[128,8,640]{2,0,1:T(8,128)(2,1)S(1)}, u32[]{:S(2)}, u32[]{:S(2)}) async-start(bf16[128,8,640]{2,0,1:T(8,128)(2,1)} %bitcast.90), calls=%async_computation.2 | async-start | bytes 2621440 | tf_op jit(solution)/shard_map/all_to_all | solution.py:52
  60.5 1.9 copy-start.2
  62.4 60.1 %collective-permute-start = (bf16[2,1024,640]{2,1,0:T(8,128)(2,1)}, bf16[2,1024,640]{2,1,0:T(8,128)(2,1)}, u32[]{:S(2)}, u32[]{:S(2)}) collective-permute-start(bf16[2,1024,640]{2,1,0:T(8,128)(2,1)} %pad_maximum_fusion), channel_id=1, source_target_pairs={{0,8},{8,16},{16,24},{24,32},{32,40},{40,48},{48,56},{56,64},{64,7... | collective-permute-start | bytes 7864328 | tf_op jit(solution)/shard_map/ppermute | solution.py:12
  70.5 7.8 %copy-start.6 = (bf16[64,5120]{1,0:T(8,128)(2,1)S(1)}, bf16[64,5120]{1,0:T(8,128)(2,1)}, u32[]{:S(2)}) copy-start(bf16[64,5120]{1,0:T(8,128)(2,1)} %param.17) | copy-start | bytes 1966084
  70.5 43.7 %all-to-all-start.3 = ((bf16[128,8,640]{0,2,1:T(8,128)(2,1)}), bf16[128,8,640]{0,2,1:T(8,128)(2,1)}, u32[]{:S(2)}, u32[]{:S(2)}) async-start(bf16[128,8,640]{0,2,1:T(8,128)(2,1)} %bitcast.89), calls=%async_computation.3 | async-start | bytes 2621440 | tf_op jit(solution)/shard_map/all_to_all | solution.py:53
  76.5 1.8 copy-start.10
  114.2 24.0 %all-to-all-start = ((bf16[128,8,640]{2,0,1:T(8,128)(2,1)}), bf16[128,8,640]{2,0,1:T(8,128)(2,1)}, u32[]{:S(2)}, u32[]{:S(2)}) async-start(bf16[128,8,640]{2,0,1:T(8,128)(2,1)} %bitcast.85), calls=%async_computation | async-start | bytes 2621440 | tf_op jit(solution)/shard_map/all_to_all | solution.py:50
  122.5 2.1 copy-start.3
  149.9 2.5 copy-start.1
  170.5 2.5 copy-start.1
  191.1 2.5 copy-start.1
  211.6 2.5 copy-start.1
  232.3 2.5 copy-start.1
  245.8 2.4 copy-start.5
  245.8 33.3 %collective-permute-start.1 = (f32[1024,640]{1,0:T(8,128)}, f32[1024,640]{1,0:T(8,128)}, u32[]{:S(2)}, u32[]{:S(2)}) collective-permute-start(f32[1024,640]{1,0:T(8,128)} %get-tuple-element.180), channel_id=1, source_target_pairs={{8,0},{16,8},{24,16},{32,24},{40,32},{48,40},{56,48},{64,56},{72,6... | collective-permute-start | bytes 7864328 | tf_op jit(solution)/shard_map/ppermute | solution.py:12
  248.2 34.8 %all-to-all-start.5 = ((bf16[8,128,640]{2,1,0:T(8,128)(2,1)}), bf16[8,128,640]{2,1,0:T(8,128)(2,1)S(1)}, u32[]{:S(2)}, u32[]{:S(2)}) async-start(bf16[8,128,640]{2,1,0:T(8,128)(2,1)} %bitcast.88), calls=%async_computation.5 | async-start | bytes 2621440 | tf_op jit(solution)/shard_map/all_to_all | solution.py:93
  283.0 6.4 %copy-start.4 = (bf16[8,128,640]{2,1,0:T(8,128)(2,1)}, bf16[8,128,640]{2,1,0:T(8,128)(2,1)S(1)}, u32[]{:S(2)}) copy-start(bf16[8,128,640]{2,1,0:T(8,128)(2,1)S(1)} %all-to-all-done.5) | copy-start | bytes 3932164
  283.0 8.2 %copy-start.7 = (bf16[64,5120]{1,0:T(8,128)(2,1)S(1)}, bf16[64,5120]{1,0:T(8,128)(2,1)}, u32[]{:S(2)}) copy-start(bf16[64,5120]{1,0:T(8,128)(2,1)} %param.17) | copy-start | bytes 1966084
  283.0 17.7 %all-to-all-start.6 = ((bf16[8,128,640]{2,1,0:T(8,128)(2,1)}), bf16[8,128,640]{2,1,0:T(8,128)(2,1)}, u32[]{:S(2)}, u32[]{:S(2)}) async-start(bf16[8,128,640]{2,1,0:T(8,128)(2,1)} %bitcast.93), calls=%async_computation.6 | async-start | bytes 2621440 | tf_op jit(solution)/shard_map/all_to_all | solution.py:94
  289.4 153.6 %all-reduce.5.cloned.1.call-start = ((), (), s32[]{:S(2)}) async-start(), calls=%async_computation.7 | async-start | bytes 10485760 | tf_op jit(solution)/shard_map/psum | solution.py:107
  291.6 11.0 %copy-start.8 = (bf16[64,5120]{1,0:T(8,128)(2,1)S(1)}, bf16[64,5120]{1,0:T(8,128)(2,1)}, u32[]{:S(2)}) copy-start(bf16[64,5120]{1,0:T(8,128)(2,1)} %param.19) | copy-start | bytes 1966084
  306.6 18.8 %all-to-all-start.4 = ((bf16[8,128,640]{2,1,0:T(8,128)(2,1)}), bf16[8,128,640]{2,1,0:T(8,128)(2,1)S(1)}, u32[]{:S(2)}, u32[]{:S(2)}) async-start(bf16[8,128,640]{2,1,0:T(8,128)(2,1)} %bitcast.87), calls=%async_computation.4 | async-start | bytes 2621440 | tf_op jit(solution)/shard_map/all_to_all | solution.py:92
Sparse Core Ops, SparseCore 0:
  306.7 136.2 all-reduce.4
